TPU v7x, 32 devices: a whole 2x2x4 slice. The times are simulated.
32 devices in a mesh: dp: 16 (over z, y, x), tensor: 2 (over core).
Axes of the slice: x: 2, y: 2, z: 4, core: 2. Of those that a mesh axis runs over, the one named last changes fastest.
Arguments:
- inputs: bfloat16 [8192, 2048], P('dp'), may hold values from -6 to 6
- gamma_first: bfloat16 [2048], replicated, may hold values from 0.099609375 to 1.8984375
- beta_first: bfloat16 [2048], replicated, may hold values from -4 to 4
- heads_weight: bfloat16 [2048, 3, 2048], P('dp', None, 'tensor'), may hold values from -0.125 to 0.125
- output_weight: bfloat16 [2048, 2048], P('dp', 'tensor'), may hold values from -0.5 to 0.5
- output_bias: bfloat16 [2048], replicated, may hold values from -4 to 4
- gamma_second: bfloat16 [2048], replicated, may hold values from 0.099609375 to 1.8984375
- beta_second: bfloat16 [2048], replicated, may hold values from -4 to 4
- expand_weight: bfloat16 [2048, 8192], P('dp', 'tensor'), may hold values from -0.125 to 0.125
- expand_bias: bfloat16 [8192], P('tensor'), may hold values from -6 to 6
- reduce_weight: bfloat16 [2048, 8192], P('dp', 'tensor'), may hold values from -0.0625 to 0.0625
- reduce_bias: bfloat16 [2048], replicated, may hold values from -4 to 4
- group_sizes: int32 [32], P('dp'), may hold values from 4 to 16, as said below
- prefix_lengths: int32 [32], P('dp'), may hold values from 32 to 128, as said below
- solution_lengths: int32 [32, 16], P('dp'), may hold values from 1 to 221, as said below
- cotangent: bfloat16 [8192, 2048], P('dp'), may hold values from -6 to 6
Outputs:
- outputs: bfloat16 [8192, 2048], P('dp')
- input_gradient: bfloat16 [8192, 2048], P('dp')
- gamma_first_gradient: float32 [2048], P('dp')
- beta_first_gradient: float32 [2048], P('dp')
- heads_weight_gradient: float32 [2048, 3, 2048], P('dp', None, 'tensor')
- output_weight_gradient: float32 [2048, 2048], P('dp', 'tensor')
- output_bias_gradient: float32 [2048], P('dp')
- gamma_second_gradient: float32 [2048], P('dp')
- beta_second_gradient: float32 [2048], P('dp')
- expand_weight_gradient: float32 [2048, 8192], P('dp', 'tensor')
- expand_bias_gradient: float32 [2, 4096], P('tensor', 'dp')
- reduce_weight_gradient: float32 [2048, 8192], P('dp', 'tensor')
- reduce_bias_gradient: float32 [2048], P('dp')
Inputs may be any that keep to these rules, and one draw needn't show every extreme that they name: Each group has group_sizes solutions. `prefix_lengths`: A group's prefix and its first group_sizes solutions together take at most 256 token slots. `solution_lengths`: only a group's first group_sizes entries are used. The groups of a block fill at most 512 slots, and on at least one block exactly 512.
All inputs are finite; a program needn't handle non-finite values.
Results may differ from a plain program's by a relative error of at most 0.017.
Values may be sent and summed in bfloat16 or wider, within the bound.
No kernel may reach another device: no remote copies, remote signals or barrier semaphores. Data moves between devices by JAX's collectives and lax.ppermute only.
A program may use at most 384 MiB of HBM per device.

v0:
```python
import jax
import jax.numpy as jnp
from jax import lax
from jax.sharding import PartitionSpec as P

HEAD = 128


def layout(group_sizes, prefix_lengths, solution_lengths, row_count):
    entries = solution_lengths.shape[1]
    position = jnp.arange(entries, dtype=jnp.int32)
    counted = jnp.where(position[None, :] < group_sizes[:, None], solution_lengths, 0)
    pieces = jnp.concatenate([prefix_lengths[:, None], counted], axis=1).reshape(-1)
    bounds = jnp.cumsum(pieces)
    slot_index = jnp.arange(row_count, dtype=jnp.int32)
    piece_index = jnp.sum((slot_index[:, None] >= bounds[None, :]).astype(jnp.int32), axis=1)
    live_rows = piece_index < pieces.shape[0]
    group_index = piece_index // (entries + 1)
    opening = piece_index % (entries + 1) == 0
    same_group = (
        (group_index[:, None] == group_index[None, :]) & live_rows[:, None] & live_rows[None, :]
    )
    causal = slot_index[None, :] <= slot_index[:, None]
    visible = opening[None, :] | (piece_index[:, None] == piece_index[None, :])
    allowed = (slot_index[:, None] == slot_index[None, :]) | same_group & causal & visible
    return (allowed, live_rows)


def normalize(values, gain_vector, shift_vector):
    center = values - jnp.mean(values, axis=-1, keepdims=True)
    spread = jnp.mean(center * center, axis=-1, keepdims=True)
    return center * lax.rsqrt(spread + 1e-05) * gain_vector + shift_vector


def smooth(values):
    return jax.nn.gelu(values, approximate=True)


def body(
    inputs,
    gamma_first,
    beta_first,
    heads_weight,
    output_weight,
    output_bias,
    gamma_second,
    beta_second,
    expand_weight,
    expand_bias,
    reduce_weight,
    reduce_bias,
    group_sizes,
    prefix_lengths,
    solution_lengths,
    cotangent,
):
    row_count = inputs.shape[0]
    local_width = output_weight.shape[1]
    local_heads = local_width // HEAD
    score_scale = HEAD ** (-0.5)
    across = (((1,), (1,)), ((), ()))
    token_dims = (((0,), (0,)), ((), ()))
    allowed, live_rows = layout(group_sizes, prefix_lengths, solution_lengths, row_count)
    live_mask = live_rows.astype(jnp.float32)[:, None]
    gain_first = gamma_first.astype(jnp.float32)
    shift_first = beta_first.astype(jnp.float32)
    gain_second = gamma_second.astype(jnp.float32)
    shift_second = beta_second.astype(jnp.float32)
    residual = inputs.astype(jnp.float32)
    first_low = normalize(residual, gain_first, shift_first).astype(jnp.bfloat16)
    heads_full, output_full = (
        lax.all_gather(heads_weight, "dp", axis=0, tiled=True),
        lax.all_gather(output_weight, "dp", axis=0, tiled=True),
    )
    projected = jnp.einsum(
        "td,dch->tch", first_low, heads_full, preferred_element_type=jnp.float32
    ).astype(jnp.bfloat16)
    queries = projected[:, 0].reshape(row_count, local_heads, HEAD)
    keyset = projected[:, 1].reshape(row_count, local_heads, HEAD)
    valueset = projected[:, 2].reshape(row_count, local_heads, HEAD)

    def masked_scores():
        raw_scores = (
            jnp.einsum("qhe,khe->hqk", queries, keyset, preferred_element_type=jnp.float32)
            * score_scale
        )
        return jnp.where(allowed[None], raw_scores, -1e30)

    scores = masked_scores()
    row_peak = jnp.max(scores, axis=-1, keepdims=True)
    exponent = jnp.exp(scores - row_peak)
    row_total = jnp.sum(exponent, axis=-1, keepdims=True)
    soft_weights = exponent / row_total
    log_total = row_peak + jnp.log(row_total)
    soft_low = soft_weights.astype(jnp.bfloat16)
    mixed_heads = (
        jnp.einsum("hqk,khe->qhe", soft_low, valueset, preferred_element_type=jnp.float32)
        .reshape(row_count, local_width)
        .astype(jnp.bfloat16)
    )
    attended = lax.psum(
        lax.dot_general(mixed_heads, output_full, across, preferred_element_type=jnp.float32),
        "tensor",
    )
    middle = residual + attended + output_bias.astype(jnp.float32)
    second_low = normalize(middle, gain_second, shift_second).astype(jnp.bfloat16)
    columns = second_low
    hidden_sum = jnp.dot(
        columns,
        lax.all_gather(expand_weight, "dp", axis=0, tiled=True),
        preferred_element_type=jnp.float32,
    ) + expand_bias.astype(jnp.float32)
    hidden_low = smooth(hidden_sum).astype(jnp.bfloat16)
    branch = lax.psum(
        lax.dot_general(
            hidden_low,
            lax.all_gather(reduce_weight, "dp", axis=0, tiled=True),
            across,
            preferred_element_type=jnp.float32,
        ).astype(jnp.bfloat16),
        "tensor",
    ).astype(jnp.float32)
    outputs = (live_mask * (middle + branch + reduce_bias.astype(jnp.float32))).astype(jnp.bfloat16)
    upstream = live_mask * cotangent.astype(jnp.float32)
    reduce_bias_gradient = jnp.sum(upstream, axis=0)
    upstream_low = upstream.astype(jnp.bfloat16)
    columns = upstream_low
    hidden_tangent = jnp.dot(
        columns,
        lax.all_gather(reduce_weight, "dp", axis=0, tiled=True),
        preferred_element_type=jnp.float32,
    )
    _, smooth_pullback = jax.vjp(smooth, hidden_sum)
    sum_tangent = smooth_pullback(hidden_tangent)[0]
    expand_bias_gradient = jnp.sum(sum_tangent, axis=0)[None, :]
    sum_low = sum_tangent.astype(jnp.bfloat16)
    second_tangent = lax.psum(
        lax.dot_general(
            sum_low,
            lax.all_gather(expand_weight, "dp", axis=0, tiled=True),
            across,
            preferred_element_type=jnp.float32,
        ).astype(jnp.bfloat16),
        "tensor",
    ).astype(jnp.float32)
    feed_totals = lax.psum_scatter(
        jnp.stack(
            [
                lax.dot_general(
                    second_low, sum_low, token_dims, preferred_element_type=jnp.float32
                ),
                lax.dot_general(
                    upstream_low, hidden_low, token_dims, preferred_element_type=jnp.float32
                ),
            ],
            axis=1,
        ),
        "dp",
        scatter_dimension=0,
        tiled=True,
    )
    expand_share = feed_totals[:, 0]
    reduce_share = feed_totals[:, 1]
    _, second_pullback = jax.vjp(normalize, middle, gain_second, shift_second)
    middle_part, gamma_second_gradient, beta_second_gradient = second_pullback(second_tangent)
    middle_tangent = upstream + middle_part
    output_bias_gradient = jnp.sum(middle_tangent, axis=0)
    middle_low = middle_tangent.astype(jnp.bfloat16)
    mixed_tangent = (
        jnp.dot(middle_low, output_full, preferred_element_type=jnp.float32)
        .astype(jnp.bfloat16)
        .reshape(row_count, local_heads, HEAD)
    )
    soft_again = jnp.exp(masked_scores() - log_total)
    soft_again_low = soft_again.astype(jnp.bfloat16)
    value_tangent = jnp.einsum(
        "hqk,qhe->khe", soft_again_low, mixed_tangent, preferred_element_type=jnp.float32
    )
    weight_tangent = jnp.einsum(
        "qhe,khe->hqk", mixed_tangent, valueset, preferred_element_type=jnp.float32
    )
    score_tangent = (
        soft_again * (weight_tangent - jnp.sum(soft_again * weight_tangent, axis=-1, keepdims=True))
    ).astype(jnp.bfloat16)
    query_tangent = (
        jnp.einsum("hqk,khe->qhe", score_tangent, keyset, preferred_element_type=jnp.float32)
        * score_scale
    )
    key_tangent = (
        jnp.einsum("hqk,qhe->khe", score_tangent, queries, preferred_element_type=jnp.float32)
        * score_scale
    )
    projected_tangent = (
        jnp.stack([query_tangent, key_tangent, value_tangent], axis=1)
        .reshape(row_count, 3, local_width)
        .astype(jnp.bfloat16)
    )
    first_tangent = lax.psum(
        jnp.einsum(
            "tch,dch->td", projected_tangent, heads_full, preferred_element_type=jnp.float32
        ).astype(jnp.bfloat16),
        "tensor",
    ).astype(jnp.float32)
    heads_term = jnp.einsum(
        "tc,tkh->ckh", first_low, projected_tangent, preferred_element_type=jnp.float32
    )
    output_term = lax.dot_general(
        middle_low, mixed_heads, token_dims, preferred_element_type=jnp.float32
    )
    head_totals = lax.psum_scatter(
        jnp.concatenate([heads_term, output_term[:, None, :]], axis=1),
        "dp",
        scatter_dimension=0,
        tiled=True,
    )
    _, first_pullback = jax.vjp(normalize, residual, gain_first, shift_first)
    input_part, gamma_first_gradient, beta_first_gradient = first_pullback(first_tangent)
    input_gradient = (middle_tangent + input_part).astype(jnp.bfloat16)
    vectors = (
        lax.psum_scatter(gamma_first_gradient, "dp", scatter_dimension=0, tiled=True),
        lax.psum_scatter(beta_first_gradient, "dp", scatter_dimension=0, tiled=True),
        lax.psum_scatter(output_bias_gradient, "dp", scatter_dimension=0, tiled=True),
        lax.psum_scatter(gamma_second_gradient, "dp", scatter_dimension=0, tiled=True),
        lax.psum_scatter(beta_second_gradient, "dp", scatter_dimension=0, tiled=True),
        lax.psum_scatter(reduce_bias_gradient, "dp", scatter_dimension=0, tiled=True),
        lax.psum_scatter(expand_bias_gradient, "dp", scatter_dimension=1, tiled=True),
    )
    return (
        outputs,
        input_gradient,
        vectors[0],
        vectors[1],
        head_totals[:, :3],
        head_totals[:, 3],
        vectors[2],
        vectors[3],
        vectors[4],
        expand_share,
        vectors[6],
        reduce_share,
        vectors[5],
    )


def solution(mesh):
    placed = (
        P("dp", None),
        P(),
        P(),
        P("dp", None, "tensor"),
        P("dp", "tensor"),
        P(),
        P(),
        P(),
        P("dp", "tensor"),
        P("tensor"),
        P("dp", "tensor"),
        P(),
        P("dp"),
        P("dp"),
        P("dp", None),
        P("dp", None),
    )
    return jax.shard_map(
        body,
        mesh=mesh,
        in_specs=placed,
        out_specs=(
            P("dp", None),
            P("dp", None),
            P("dp"),
            P("dp"),
            P("dp", None, "tensor"),
            P("dp", "tensor"),
            P("dp"),
            P("dp"),
            P("dp"),
            P("dp", "tensor"),
            P("tensor", "dp"),
            P("dp", "tensor"),
            P("dp"),
        ),
        check_vma=False,
    )
```

profile of v0, /device:TPU:10, one launch (start us, length us, event | category | flops | bytes accessed | tf_op | source)
XLA Modules:
  0.0 2903.4 jit_solution(15388383072456782599)
XLA Ops:
  16.1 145.8 %all-gather.5.cloned.1.call-done = bf16[2048,3,1024]{2,0,1:T(8,128)(2,1)} async-done(((bf16[128,3,1024]{2,0,1:T(8,128)(2,1)}), bf16[2048,3,1024]{2,0,1:T(8,128)(2,1)}) %all-gather.5.cloned.1.call-update) | async-done | bytes 12582928 | tf_op jit(solution)/shard_map/all_gather | solution.py:72
  162.0 9.7 convolution_convert_fusion.2
  187.9 53.0 %all-gather.7.cloned.1.call-done = bf16[2048,1024]{1,0:T(8,128)(2,1)} async-done(((bf16[128,1024]{1,0:T(8,128)(2,1)}), bf16[2048,1024]{1,0:T(8,128)(2,1)}) %all-gather.7.cloned.1.call-update) | async-done | bytes 4194320 | tf_op jit(solution)/shard_map/all_gather | solution.py:73
  240.9 6.8 fusion.68
  249.2 26.0 all-reduce.12.cloned.1.call-done
  280.6 188.2 %all-gather.9.cloned.1.call-done = bf16[2048,4096]{1,0:T(8,128)(2,1)} async-done(((bf16[128,4096]{1,0:T(8,128)(2,1)}), bf16[2048,4096]{1,0:T(8,128)(2,1)}) %all-gather.9.cloned.1.call-update) | async-done | bytes 16777232 | tf_op jit(solution)/shard_map/all_gather | solution.py:110
  468.9 15.8 fusion.61
  484.7 177.0 %all-gather.11.cloned.1.call-done = bf16[2048,4096]{1,0:T(8,128)(2,1)} async-done(((bf16[128,4096]{1,0:T(8,128)(2,1)}), bf16[2048,4096]{1,0:T(8,128)(2,1)}) %all-gather.11.cloned.1.call-update) | async-done | bytes 16777232 | tf_op jit(solution)/shard_map/all_gather | solution.py:117
  661.7 18.5 fusion.67
  682.2 13.4 convolution_convert_fusion
  697.7 18.8 convolution_convert_fusion.1
  732.3 5.1 fusion.35
  737.4 4.8 multiply_reduce_fusion
  750.3 11.3 bitcast_convert_fusion
  761.8 5.1 convolution_bitcast_fusion.2
  767.0 12.0 fusion.38
  779.0 20.2 pad_maximum_fusion.1
  799.9 20.1 convolution_bitcast_fusion.1
  820.1 19.7 convolution_bitcast_fusion
  839.8 44.5 %pad_maximum_fusion = f32[2048,2,4096]{2,0,1:T(8,128)} fusion(f32[2048,1,4096]{2,0,1:T(8,128)} %convolution_bitcast_fusion, f32[2048,1,4096]{2,0,1:T(8,128)} %convolution_bitcast_fusion.1), kind=kLoop, calls=%fused_computation | loop fusion | flops 16777216 | bytes 134217728 | tf_op jit(solution)/shard_map/stack | solution.py:147
  893.3 71.1 %all-reduce.6 = (f32[2048]{0:T(1024)S(1)}, f32[2048]{0:T(1024)S(1)}, f32[2048]{0:T(1024)S(1)}, f32[2048]{0:T(1024)S(1)}, f32[2048]{0:T(1024)S(1)}, /*index=5*/f32[2048]{0:T(1024)S(1)}) all-reduce(f32[2048]{0:T(1024)S(1)} %get-tuple-element.15, f32[2048]{0:T(1024)S(1)} %get-tuple-element.19, ...), channel_id=2, replica_groups=mesh['dp'=16,'tensor'=2] {'dp'}, use_global_device_ids=true, to_apply=%region_18.19.clone | all-reduce | flops 12288 | bytes 98304
  967.8 4.9 multiply_convert_fusion.2
  975.7 550.2 %reduce-scatter.6.cloned.1.call-done = f32[128,4,1024]{2,0,1:T(8,128)} async-done(((f32[2048,4,1024]{2,0,1:T(8,128)}), f32[128,4,1024]{2,0,1:T(8,128)}) %reduce-scatter.6.cloned.1.call-update) | async-done | bytes 2097168 | tf_op jit(solution)/shard_map/reduce_scatter | solution.py:210
  1530.5 1360.9 %reduce-scatter.8.cloned.1.call-done = f32[128,2,4096]{2,0,1:T(8,128)} async-done(((f32[2048,2,4096]{2,0,1:T(8,128)}), f32[128,2,4096]{2,0,1:T(8,128)}) %reduce-scatter.8.cloned.1.call-update) | async-done | bytes 4194320 | tf_op jit(solution)/shard_map/reduce_scatter | solution.py:146
  (181 shorter events, 84.2 us)
Async XLA Ops:
  7.2 6.8 copy-start.3
  7.2 154.8 %all-gather.5.cloned.1.call-start = ((), (), s32[]{:S(2)}) async-start(), calls=%async_computation.3 | async-start | bytes 13369344 | tf_op jit(solution)/shard_map/all_gather | solution.py:72
  7.9 232.9 %all-gather.7.cloned.1.call-start = ((), (), s32[]{:S(2)}) async-start(), calls=%async_computation.4 | async-start | bytes 4456448 | tf_op jit(solution)/shard_map/all_gather | solution.py:73
  8.7 266.5 %all-reduce.12.cloned.1.call-start = ((), (), s32[]{:S(2)}) async-start(), calls=%async_computation.5 | async-start | bytes 8388608 | tf_op jit(solution)/shard_map/psum | solution.py:101
  10.2 161.6 %copy-start.21 = (f32[2048]{0:T(1024)}, f32[2048]{0:T(1024)S(1)}, u32[]{:S(2)}) copy-start(f32[2048]{0:T(1024)S(1)} %convert_element_type.107) | copy-start | bytes 24580
  10.8 160.9 %copy-start.34 = (f32[2048]{0:T(1024)}, f32[2048]{0:T(1024)S(1)}, u32[]{:S(2)}) copy-start(f32[2048]{0:T(1024)S(1)} %convert_element_type.108) | copy-start | bytes 24580
  14.0 157.7 %copy-start.23 = (f32[512]{0:T(512)}, f32[512]{0:T(512)S(1)}, u32[]{:S(2)}) copy-start(f32[512]{0:T(512)S(1)} %broadcast_multiply_fusion.1) | copy-start | bytes 6148
  14.7 157.0 %copy-start.29 = (f32[512]{0:T(512)}, f32[512]{0:T(512)S(1)}, u32[]{:S(2)}) copy-start(f32[512]{0:T(512)S(1)} %fusion.56) | copy-start | bytes 6148
  176.2 5.6 copy-start.10
  247.7 221.2 %all-gather.9.cloned.1.call-start = ((), (), s32[]{:S(2)}) async-start(), calls=%async_computation.6 | async-start | bytes 17825792 | tf_op jit(solution)/shard_map/all_gather | solution.py:110
  248.3 413.4 %all-gather.11.cloned.1.call-start = ((), (), s32[]{:S(2)}) async-start(), calls=%async_computation.7 | async-start | bytes 17825792 | tf_op jit(solution)/shard_map/all_gather | solution.py:117
  248.9 468.4 %all-reduce.14.cloned.1.call-start = ((), (), s32[]{:S(2)}) async-start(), calls=%async_computation.8 | async-start | bytes 4194304 | tf_op jit(solution)/shard_map/psum | solution.py:137
  249.2 219.7 %copy-start.36 = (f32[2048]{0:T(1024)}, f32[2048]{0:T(1024)S(1)}, u32[]{:S(2)}) copy-start(f32[2048]{0:T(1024)S(1)} %convert_element_type.117) | copy-start | bytes 24580
  280.6 381.1 %copy-start.14 = (bf16[512,2048]{1,0:T(8,128)(2,1)S(1)}, bf16[512,2048]{1,0:T(8,128)(2,1)}, u32[]{:S(2)}) copy-start(bf16[512,2048]{1,0:T(8,128)(2,1)} %param.31) | copy-start | bytes 6291460
  695.6 190.6 %reduce-scatter.10.cloned.1.call-start = ((), (), s32[]{:S(2)}) async-start(), calls=%async_computation.11 | async-start | bytes 2228224
  697.7 190.1 %all-reduce.16.cloned.1.call-start = ((), (), s32[]{:S(2)}) async-start(), calls=%async_computation.12 | async-start | bytes 8388608 | tf_op jit(solution)/shard_map/psum | solution.py:114
  732.3 9.9 slice-start
  750.3 11.4 copy-start.19
  761.8 764.1 %reduce-scatter.6.cloned.1.call-start = ((), (), s32[]{:S(2)}) async-start(), calls=%async_computation.9 | async-start | bytes 35651584 | tf_op jit(solution)/shard_map/reduce_scatter | solution.py:210
  799.3 2092.1 %reduce-scatter.8.cloned.1.call-start = ((), (), s32[]{:S(2)}) async-start(), calls=%async_computation.10 | async-start | bytes 71303168 | tf_op jit(solution)/shard_map/reduce_scatter | solution.py:146
  799.9 20.1 copy-start.15
  884.3 6.4 copy-start.32
  887.8 5.4 copy-start.27
  887.8 5.4 copy-start.28
  (33 other events, 111.9 us)
Sparse Core Ops, SparseCore 0:
  10.8 151.1 all-gather.4
  164.7 76.1 all-gather.6
  247.8 27.2 all-reduce.11
  278.2 190.6 all-gather.8
  471.9 189.7 all-gather.10
  695.7 21.5 all-reduce.13
  720.2 71.8 reduce-scatter.9
  795.2 35.4 all-reduce.15
  833.2 692.6 reduce-scatter.5
  1528.2 1363.1 reduce-scatter.7
where the time goes:
time: 2910 us; the launch traced here: 2900 us
  waiting for transfers between devices  2500 us (86%)
  matrix products  171 us (6%)
  other arithmetic  101 us (3%)
  blocking collectives  71.1 us (2%)
  local copies, waits for them, and re-layouts  38.9 us (1%)
    reduce_scatter x1, waiting for transfers between devices, body(): lax.psum_scatter(jnp.stack([lax.dot_general(second_low, sum_low, token_di...  1360 us
    reduce_scatter x1, waiting for transfers between devices, body(): lax.psum_scatter(jnp.concatenate([heads_term, output_term[:, None, :]], a...  550 us
    all_gather x1, waiting for transfers between devices, body(): lax.all_gather(expand_weight, 'dp', axis=0, tiled=True)  188 us
    all_gather x1, waiting for transfers between devices, body(): lax.all_gather(reduce_weight, 'dp', axis=0, tiled=True)  177 us
    all_gather x1, waiting for transfers between devices, body(): lax.all_gather(heads_weight, 'dp', axis=0, tiled=True)  146 us
    unnamed x1, blocking collectives  71.1 us
  transfers between devices with their start and end apart: 10, of which 8 were waited for; matrix products, arithmetic and copies ran while one was open for 9% of the time, Pallas kernels for 0%

commit v1 on v0

--- a/solution.py
+++ b/solution.py
@@ -4,6 +4,19 @@
 from jax.sharding import PartitionSpec as P
 
 HEAD = 128
+
+
+def ring_gather(value, axis, dim):
+    ways = lax.axis_size(axis)
+    up = [(d, (d + 1) % ways) for d in range(ways)]
+    down = [(d, (d - 1) % ways) for d in range(ways)]
+    earlier, later = ([value], [value])
+    for _ in range(ways // 2):
+        earlier.append(lax.ppermute(earlier[-1], axis, up))
+    for _ in range((ways - 1) // 2):
+        later.append(lax.ppermute(later[-1], axis, down))
+    line = jnp.concatenate([*earlier[::-1], *later[1:]], axis=dim)
+    return jnp.roll(line, (lax.axis_index(axis) - ways // 2) * value.shape[dim], axis=dim)
 
 
 def layout(group_sizes, prefix_lengths, solution_lengths, row_count):
@@ -106,9 +119,7 @@
     second_low = normalize(middle, gain_second, shift_second).astype(jnp.bfloat16)
     columns = second_low
     hidden_sum = jnp.dot(
-        columns,
-        lax.all_gather(expand_weight, "dp", axis=0, tiled=True),
-        preferred_element_type=jnp.float32,
+        columns, ring_gather(expand_weight, "dp", 0), preferred_element_type=jnp.float32
     ) + expand_bias.astype(jnp.float32)
     hidden_low = smooth(hidden_sum).astype(jnp.bfloat16)
     branch = lax.psum(

time: 2910 us -> 3110 us (1.069)
  waiting for transfers between devices: 2500 us -> 2630 us
  local copies, waits for them, and re-layouts: 38.9 us -> 81.7 us
    ppermute x0 -> x15, waiting for transfers between devices: none -> 391 us  [the longest x8 257 us: ring_gather(): earlier.append(lax.ppermute(earlier[-1], axis, up))]
    all_gather x1, waiting for transfers between devices: 177 us -> 0.01 us  [body(): lax.all_gather(reduce_weight, 'dp', axis=0, tiled=True)]
    all_gather x1, waiting for transfers between devices: 188 us -> 122 us  [body(): lax.all_gather(expand_weight, 'dp', axis=0, tiled=True)]
    unnamed x105 -> x184, local copies, waits for them, and re-layouts: 20.9 us -> 62.6 us
  transfers between devices with their start and end apart: 10 -> 25, of which waited for: 8 -> 21; matrix products, arithmetic and copies ran while one was open for 9% -> 10% of each run, Pallas kernels for 0% -> 0%
where the time goes in v1:
time: 3110 us; the launch traced here: 3100 us
  waiting for transfers between devices  2630 us (85%)
  matrix products  173 us (6%)
  other arithmetic  101 us (3%)
  local copies, waits for them, and re-layouts  81.7 us (3%)
  blocking collectives  70.9 us (2%)
    reduce_scatter x1, waiting for transfers between devices, body(): lax.psum_scatter(jnp.stack([lax.dot_general(second_low, sum_low, token_di...  1360 us
    reduce_scatter x1, waiting for transfers between devices, body(): lax.psum_scatter(jnp.concatenate([heads_term, output_term[:, None, :]], a...  550 us
    ppermute x8, waiting for transfers between devices, ring_gather(): earlier.append(lax.ppermute(earlier[-1], axis, up))  257 us
    all_gather x1, waiting for transfers between devices, body(): lax.all_gather(heads_weight, 'dp', axis=0, tiled=True)  146 us
    ppermute x7, waiting for transfers between devices, ring_gather(): later.append(lax.ppermute(later[-1], axis, down))  134 us
    all_gather x1, waiting for transfers between devices, body(): lax.all_gather(expand_weight, 'dp', axis=0, tiled=True)  122 us
    unnamed x1, blocking collectives  70.9 us
    unnamed x184, local copies, waits for them, and re-layouts  62.6 us
  transfers between devices with their start and end apart: 25, of which 21 were waited for; matrix products, arithmetic and copies ran while one was open for 10% of the time, Pallas kernels for 0%

profile of v1, /device:TPU:10, one launch (start us, length us, event | category | flops | bytes accessed | tf_op | source)
XLA Modules:
  0.0 3097.3 jit_solution(4947663843980644889)
XLA Ops:
  16.1 145.8 %all-gather.5.cloned.1.call-done = bf16[2048,3,1024]{2,0,1:T(8,128)(2,1)} async-done(((bf16[128,3,1024]{2,0,1:T(8,128)(2,1)}), bf16[2048,3,1024]{2,0,1:T(8,128)(2,1)}) %all-gather.5.cloned.1.call-update) | async-done | bytes 12582928 | tf_op jit(solution)/shard_map/all_gather | solution.py:85
  187.4 53.4 %all-gather.7.cloned.1.call-done = bf16[2048,1024]{1,0:T(8,128)(2,1)} async-done(((bf16[128,1024]{1,0:T(8,128)(2,1)}), bf16[2048,1024]{1,0:T(8,128)(2,1)}) %all-gather.7.cloned.1.call-update) | async-done | bytes 4194320 | tf_op jit(solution)/shard_map/all_gather | solution.py:86
  250.4 22.2 collective-permute-done
  275.1 51.3 %collective-permute-done.1 = bf16[128,4096]{1,0:T(8,128)(2,1)S(1)} collective-permute-done((bf16[128,4096]{1,0:T(8,128)(2,1)S(1)}, bf16[128,4096]{1,0:T(8,128)(2,1)S(1)}, u32[]{:S(2)}, u32[]{:S(2)}) %collective-permute-start.1) | collective-permute-done | bytes 1048608 | tf_op jit(solution)/shard_map/ppermute | solution.py:15
  330.1 60.8 %collective-permute-done.2 = bf16[128,4096]{1,0:T(8,128)(2,1)S(1)} collective-permute-done((bf16[128,4096]{1,0:T(8,128)(2,1)S(1)}, bf16[128,4096]{1,0:T(8,128)(2,1)S(1)}, u32[]{:S(2)}, u32[]{:S(2)}) %collective-permute-start.2) | collective-permute-done | bytes 1048608 | tf_op jit(solution)/shard_map/ppermute | solution.py:15
  405.0 19.8 collective-permute-done.3
  428.2 19.2 collective-permute-done.10
  449.8 22.7 collective-permute-done.4
  475.8 44.8 %collective-permute-done.11 = bf16[128,4096]{1,0:T(8,128)(2,1)S(1)} collective-permute-done((bf16[128,4096]{1,0:T(8,128)(2,1)S(1)}, bf16[128,4096]{1,0:T(8,128)(2,1)S(1)}, u32[]{:S(2)}, u32[]{:S(2)}) %collective-permute-start.11) | collective-permute-done | bytes 1048608 | tf_op jit(solution)/shard_map/ppermute | solution.py:17
  521.7 40.7 %collective-permute-done.5 = bf16[128,4096]{1,0:T(8,128)(2,1)S(1)} collective-permute-done((bf16[128,4096]{1,0:T(8,128)(2,1)S(1)}, bf16[128,4096]{1,0:T(8,128)(2,1)S(1)}, u32[]{:S(2)}, u32[]{:S(2)}) %collective-permute-start.5) | collective-permute-done | bytes 1048608 | tf_op jit(solution)/shard_map/ppermute | solution.py:15
  565.7 31.3 %collective-permute-done.12 = bf16[128,4096]{1,0:T(8,128)(2,1)} collective-permute-done((bf16[128,4096]{1,0:T(8,128)(2,1)S(1)}, bf16[128,4096]{1,0:T(8,128)(2,1)}, u32[]{:S(2)}, u32[]{:S(2)}) %collective-permute-start.12) | collective-permute-done | bytes 1048608 | tf_op jit(solution)/shard_map/ppermute | solution.py:17
  599.6 19.9 collective-permute-done.6
  623.1 19.0 collective-permute-done.13
  644.6 20.0 collective-permute-done.7
  732.4 19.9 fusion.69
  752.2 122.0 %all-gather.11.cloned.1.call-done = bf16[2048,4096]{1,0:T(8,128)(2,1)} async-done(((bf16[128,4096]{1,0:T(8,128)(2,1)}), bf16[2048,4096]{1,0:T(8,128)(2,1)}) %all-gather.11.cloned.1.call-update) | async-done | bytes 16777232 | tf_op jit(solution)/shard_map/all_gather | solution.py:151
  891.4 18.3 convolution_convert_fusion.1
  974.7 20.3 pad_maximum_fusion.1
  995.1 20.4 convolution_bitcast_fusion
  1015.5 18.6 convolution_bitcast_fusion.1
  1034.1 44.3 %pad_maximum_fusion = f32[2048,2,4096]{2,0,1:T(8,128)} fusion(f32[2048,1,4096]{2,0,1:T(8,128)} %convolution_bitcast_fusion, f32[2048,1,4096]{2,0,1:T(8,128)} %convolution_bitcast_fusion.1), kind=kLoop, calls=%fused_computation | loop fusion | flops 16777216 | bytes 134217728 | tf_op jit(solution)/shard_map/stack | solution.py:158
  1087.4 70.9 %all-reduce.6 = (f32[2048]{0:T(1024)S(1)}, f32[2048]{0:T(1024)S(1)}, f32[2048]{0:T(1024)S(1)}, f32[2048]{0:T(1024)S(1)}, f32[2048]{0:T(1024)S(1)}, /*index=5*/f32[2048]{0:T(1024)S(1)}) all-reduce(f32[2048]{0:T(1024)S(1)} %get-tuple-element.15, f32[2048]{0:T(1024)S(1)} %get-tuple-element.19, ...), channel_id=2, replica_groups=mesh['dp'=16,'tensor'=2] {'dp'}, use_global_device_ids=true, to_apply=%region_18.19.clone | all-reduce | flops 12288 | bytes 98304
  1169.6 550.2 %reduce-scatter.6.cloned.1.call-done = f32[128,4,1024]{2,0,1:T(8,128)} async-done(((f32[2048,4,1024]{2,0,1:T(8,128)}), f32[128,4,1024]{2,0,1:T(8,128)}) %reduce-scatter.6.cloned.1.call-update) | async-done | bytes 2097168 | tf_op jit(solution)/shard_map/reduce_scatter | solution.py:221
  1724.4 1360.9 %reduce-scatter.8.cloned.1.call-done = f32[128,2,4096]{2,0,1:T(8,128)} async-done(((f32[2048,2,4096]{2,0,1:T(8,128)}), f32[128,2,4096]{2,0,1:T(8,128)}) %reduce-scatter.8.cloned.1.call-update) | async-done | bytes 4194320 | tf_op jit(solution)/shard_map/reduce_scatter | solution.py:157
  (291 shorter events, 264.5 us)
Async XLA Ops:
  7.2 154.8 %all-gather.5.cloned.1.call-start = ((), (), s32[]{:S(2)}) async-start(), calls=%async_computation.3 | async-start | bytes 13369344 | tf_op jit(solution)/shard_map/all_gather | solution.py:85
  7.9 232.9 %all-gather.7.cloned.1.call-start = ((), (), s32[]{:S(2)}) async-start(), calls=%async_computation.4 | async-start | bytes 4456448 | tf_op jit(solution)/shard_map/all_gather | solution.py:86
  8.7 704.0 %all-reduce.12.cloned.1.call-start = ((), (), s32[]{:S(2)}) async-start(), calls=%async_computation.5 | async-start | bytes 8388608 | tf_op jit(solution)/shard_map/psum | solution.py:114
  247.5 484.9 %all-gather.9.cloned.1.call-start = ((), (), s32[]{:S(2)}) async-start(), calls=%async_computation.6 | async-start | bytes 17825792 | tf_op jit(solution)/shard_map/all_gather | solution.py:128
  248.1 626.2 %all-gather.11.cloned.1.call-start = ((), (), s32[]{:S(2)}) async-start(), calls=%async_computation.7 | async-start | bytes 17825792 | tf_op jit(solution)/shard_map/all_gather | solution.py:151
  248.6 662.3 %all-reduce.14.cloned.1.call-start = ((), (), s32[]{:S(2)}) async-start(), calls=%async_computation.8 | async-start | bytes 4194304 | tf_op jit(solution)/shard_map/psum | solution.py:148
  272.7 53.6 %collective-permute-start.1 = (bf16[128,4096]{1,0:T(8,128)(2,1)S(1)}, bf16[128,4096]{1,0:T(8,128)(2,1)S(1)}, u32[]{:S(2)}, u32[]{:S(2)}) collective-permute-start(bf16[128,4096]{1,0:T(8,128)(2,1)S(1)} %collective-permute-done), channel_id=1, source_target_pairs={{0,2},{2,4},{4,6},{6,8},{8,10},{10,12},{12,14},{14,16},{16,18},{18... | collective-permute-start | bytes 3145736 | tf_op jit(solution)/shard_map/ppermute | solution.py:15
  275.1 54.0 %collective-permute-start.8 = (bf16[128,4096]{1,0:T(8,128)(2,1)S(1)}, bf16[128,4096]{1,0:T(8,128)(2,1)S(1)}, u32[]{:S(2)}, u32[]{:S(2)}) collective-permute-start(bf16[128,4096]{1,0:T(8,128)(2,1)S(1)} %copy-done.11), channel_id=1, source_target_pairs={{0,30},{2,0},{4,2},{6,4},{8,6},{10,8},{12,10},{14,12},{16,14},{18,... | collective-permute-start | bytes 3145736 | tf_op jit(solution)/shard_map/ppermute | solution.py:17
  326.3 64.5 %collective-permute-start.2 = (bf16[128,4096]{1,0:T(8,128)(2,1)S(1)}, bf16[128,4096]{1,0:T(8,128)(2,1)S(1)}, u32[]{:S(2)}, u32[]{:S(2)}) collective-permute-start(bf16[128,4096]{1,0:T(8,128)(2,1)S(1)} %collective-permute-done.1), channel_id=1, source_target_pairs={{0,2},{2,4},{4,6},{6,8},{8,10},{10,12},{12,14},{14,16},{16,18},{18... | collective-permute-start | bytes 3145736 | tf_op jit(solution)/shard_map/ppermute | solution.py:15
  329.1 74.9 %collective-permute-start.9 = (bf16[128,4096]{1,0:T(8,128)(2,1)S(1)}, bf16[128,4096]{1,0:T(8,128)(2,1)S(1)}, u32[]{:S(2)}, u32[]{:S(2)}) collective-permute-start(bf16[128,4096]{1,0:T(8,128)(2,1)S(1)} %collective-permute-done.8), channel_id=1, source_target_pairs={{0,30},{2,0},{4,2},{6,4},{8,6},{10,8},{12,10},{14,12},{16,14},{18,... | collective-permute-start | bytes 3145736 | tf_op jit(solution)/shard_map/ppermute | solution.py:17
  390.9 34.0 %collective-permute-start.3 = (bf16[128,4096]{1,0:T(8,128)(2,1)S(1)}, bf16[128,4096]{1,0:T(8,128)(2,1)S(1)}, u32[]{:S(2)}, u32[]{:S(2)}) collective-permute-start(bf16[128,4096]{1,0:T(8,128)(2,1)S(1)} %collective-permute-done.2), channel_id=1, source_target_pairs={{0,2},{2,4},{4,6},{6,8},{8,10},{10,12},{12,14},{14,16},{16,18},{18... | collective-permute-start | bytes 3145736 | tf_op jit(solution)/shard_map/ppermute | solution.py:15
  404.0 43.4 %collective-permute-start.10 = (bf16[128,4096]{1,0:T(8,128)(2,1)S(1)}, bf16[128,4096]{1,0:T(8,128)(2,1)S(1)}, u32[]{:S(2)}, u32[]{:S(2)}) collective-permute-start(bf16[128,4096]{1,0:T(8,128)(2,1)S(1)} %collective-permute-done.9), channel_id=1, source_target_pairs={{0,30},{2,0},{4,2},{6,4},{8,6},{10,8},{12,10},{14,12},{16,14},{18,... | collective-permute-start | bytes 3145736 | tf_op jit(solution)/shard_map/ppermute | solution.py:17
  424.8 47.6 %collective-permute-start.4 = (bf16[128,4096]{1,0:T(8,128)(2,1)S(1)}, bf16[128,4096]{1,0:T(8,128)(2,1)S(1)}, u32[]{:S(2)}, u32[]{:S(2)}) collective-permute-start(bf16[128,4096]{1,0:T(8,128)(2,1)S(1)} %collective-permute-done.3), channel_id=1, source_target_pairs={{0,2},{2,4},{4,6},{6,8},{8,10},{10,12},{12,14},{14,16},{16,18},{18... | collective-permute-start | bytes 3145736 | tf_op jit(solution)/shard_map/ppermute | solution.py:15
  447.4 73.2 %collective-permute-start.11 = (bf16[128,4096]{1,0:T(8,128)(2,1)S(1)}, bf16[128,4096]{1,0:T(8,128)(2,1)S(1)}, u32[]{:S(2)}, u32[]{:S(2)}) collective-permute-start(bf16[128,4096]{1,0:T(8,128)(2,1)S(1)} %collective-permute-done.10), channel_id=1, source_target_pairs={{0,30},{2,0},{4,2},{6,4},{8,6},{10,8},{12,10},{14,12},{16,14},{18,... | collective-permute-start | bytes 3145736 | tf_op jit(solution)/shard_map/ppermute | solution.py:17
  472.5 89.9 %collective-permute-start.5 = (bf16[128,4096]{1,0:T(8,128)(2,1)S(1)}, bf16[128,4096]{1,0:T(8,128)(2,1)S(1)}, u32[]{:S(2)}, u32[]{:S(2)}) collective-permute-start(bf16[128,4096]{1,0:T(8,128)(2,1)S(1)} %collective-permute-done.4), channel_id=1, source_target_pairs={{0,2},{2,4},{4,6},{6,8},{8,10},{10,12},{12,14},{14,16},{16,18},{18... | collective-permute-start | bytes 3145736 | tf_op jit(solution)/shard_map/ppermute | solution.py:15
  521.7 75.4 %collective-permute-start.12 = (bf16[128,4096]{1,0:T(8,128)(2,1)S(1)}, bf16[128,4096]{1,0:T(8,128)(2,1)}, u32[]{:S(2)}, u32[]{:S(2)}) collective-permute-start(bf16[128,4096]{1,0:T(8,128)(2,1)S(1)} %collective-permute-done.11), channel_id=1, source_target_pairs={{0,30},{2,0},{4,2},{6,4},{8,6},{10,8},{12,10},{14,12},{16,14},{18,... | collective-permute-start | bytes 3145736 | tf_op jit(solution)/shard_map/ppermute | solution.py:17
  562.3 57.2 %collective-permute-start.6 = (bf16[128,4096]{1,0:T(8,128)(2,1)S(1)}, bf16[128,4096]{1,0:T(8,128)(2,1)}, u32[]{:S(2)}, u32[]{:S(2)}) collective-permute-start(bf16[128,4096]{1,0:T(8,128)(2,1)S(1)} %collective-permute-done.5), channel_id=1, source_target_pairs={{0,2},{2,4},{4,6},{6,8},{8,10},{10,12},{12,14},{14,16},{16,18},{18... | collective-permute-start | bytes 3145736 | tf_op jit(solution)/shard_map/ppermute | solution.py:15
  597.0 45.0 %collective-permute-start.13 = (bf16[128,4096]{1,0:T(8,128)(2,1)}, bf16[128,4096]{1,0:T(8,128)(2,1)}, u32[]{:S(2)}, u32[]{:S(2)}) collective-permute-start(bf16[128,4096]{1,0:T(8,128)(2,1)} %collective-permute-done.12), channel_id=1, source_target_pairs={{0,30},{2,0},{4,2},{6,4},{8,6},{10,8},{12,10},{14,12},{16,14},{18,... | collective-permute-start | bytes 3145736 | tf_op jit(solution)/shard_map/ppermute | solution.py:17
  619.5 45.0 %collective-permute-start.7 = (bf16[128,4096]{1,0:T(8,128)(2,1)}, bf16[128,4096]{1,0:T(8,128)(2,1)}, u32[]{:S(2)}, u32[]{:S(2)}) collective-permute-start(bf16[128,4096]{1,0:T(8,128)(2,1)} %collective-permute-done.6), channel_id=1, source_target_pairs={{0,2},{2,4},{4,6},{6,8},{8,10},{10,12},{12,14},{14,16},{16,18},{18... | collective-permute-start | bytes 3145736 | tf_op jit(solution)/shard_map/ppermute | solution.py:15
  642.1 47.4 %collective-permute-start.14 = (bf16[128,4096]{1,0:T(8,128)(2,1)}, bf16[128,4096]{1,0:T(8,128)(2,1)S(1)}, u32[]{:S(2)}, u32[]{:S(2)}) collective-permute-start(bf16[128,4096]{1,0:T(8,128)(2,1)} %collective-permute-done.13), channel_id=1, source_target_pairs={{0,30},{2,0},{4,2},{6,4},{8,6},{10,8},{12,10},{14,12},{16,14},{18,... | collective-permute-start | bytes 3145736 | tf_op jit(solution)/shard_map/ppermute | solution.py:17
  889.3 191.1 %reduce-scatter.10.cloned.1.call-start = ((), (), s32[]{:S(2)}) async-start(), calls=%async_computation.11 | async-start | bytes 2228224
  891.3 190.6 %all-reduce.16.cloned.1.call-start = ((), (), s32[]{:S(2)}) async-start(), calls=%async_computation.12 | async-start | bytes 8388608 | tf_op jit(solution)/shard_map/psum | solution.py:125
  957.4 762.4 %reduce-scatter.6.cloned.1.call-start = ((), (), s32[]{:S(2)}) async-start(), calls=%async_computation.9 | async-start | bytes 35651584 | tf_op jit(solution)/shard_map/reduce_scatter | solution.py:221
  995.1 2090.2 %reduce-scatter.8.cloned.1.call-start = ((), (), s32[]{:S(2)}) async-start(), calls=%async_computation.10 | async-start | bytes 71303168 | tf_op jit(solution)/shard_map/reduce_scatter | solution.py:157
  (72 other events, 3260.0 us)
Sparse Core Ops, SparseCore 0:
  10.8 151.1 all-gather.4
  164.7 76.1 all-gather.6
  247.6 27.2 all-reduce.11
  277.9 397.7 all-gather.8
  678.8 195.4 all-gather.10
  889.4 21.5 all-reduce.13
  913.8 72.6 reduce-scatter.9
  989.6 35.0 all-reduce.15
  1027.1 692.6 reduce-scatter.5
  1722.1 1363.1 reduce-scatter.7
